TPU v7x, 512 devices: a whole 4x8x8 slice. The times are simulated.
512 devices in a mesh: grp: 4 (over z_lo, core), blk: 128 (over y, z_hi, x).
Axes of the slice: x: 4, y: 8, z: 8 (z_hi: 4, z_lo: 2; z = z_hi * 2 + z_lo), core: 2. Of those that a mesh axis runs over, the one named last changes fastest.
Arguments:
- vertices: float32 [3, 131072], P(None, ('grp', 'blk')), may hold values from -6 to 6
- faces: int32 [3, 262144], P(None, ('grp', 'blk')), may hold values from 0 to 255
- trial_step: float32 [3, 131072], P(None, ('grp', 'blk')), may hold values from -2 to 2
- accepted: int32 [4], P('grp'), may hold values from 0 to 1
- face_weight: float32 [262144], P(('grp', 'blk')), may hold values from 0.5 to 6
- partner_shift: int32 [2, 4], replicated, may hold values from 1 to 3, as said below
Outputs:
- vertex_grad: float32 [3, 131072], P(None, ('grp', 'blk'))
- energy: float32 [1], replicated
Inputs may be any that keep to these rules, and one draw needn't show every extreme that they name: `partner_shift`: for each group the 2 offsets are all different, and the first round's offset is 4 // 2 for every group.
All inputs are finite; a program needn't handle non-finite values.
Results may differ from a plain program's by a relative error of at most 0.0001.
Values sent between devices are 32-bit elements; how exact they have to be, the bound alone decides.
A program may use at most 64 MiB of HBM per device.

v0:
```python
import functools

import jax
import jax.numpy as jnp
from jax import lax
from jax.sharding import Mesh
from jax.sharding import PartitionSpec as P

HOPS = 4
BLK = ("blk_0", "blk_1", "blk_2")
GRP = ("grp_0", "grp_1")
GRP_BLK = ("grp_0", "grp_1", "blk_0", "blk_1", "blk_2")


EPS2 = 0.05


def from_behind(value, axis, by):
    count = lax.axis_size(axis)
    return lax.ppermute(value, axis, [(i, (i + by) % count) for i in range(count)])


def joined_along(parts, dim):
    parts = jnp.moveaxis(parts, 0, dim)
    lengths = parts.shape
    return parts.reshape(*lengths[:dim], lengths[dim] * lengths[dim + 1], *lengths[dim + 2 :])


def from_everyone(value, axis):
    count = lax.axis_size(axis)
    return lax.all_to_all(
        jnp.broadcast_to(value[None], (count, *value.shape)), axis, 0, 0, tiled=True
    )


def gather_directly(value, axis, dim):
    return joined_along(from_everyone(value, axis), dim)


def in_blocks(value, dim, count):
    before, after = (value.shape[:dim], value.shape[dim + 1 :])
    return jnp.moveaxis(value.reshape(*before, count, -1, *after), dim, 0)


def summed_on_arrival(value, axis, dim):
    count = lax.axis_size(axis)
    parts = lax.all_to_all(in_blocks(value, dim, count), axis, 0, 0, tiled=True)
    return jnp.sum(parts, axis=0)


def by_axis(value, axes):
    return functools.reduce(lax.psum, axes, value)


def pair_energy(own_geo, own_weight, other_geo, other_weight):
    d0 = own_geo[0][:, None] - other_geo[0][None, :]
    d1 = own_geo[1][:, None] - other_geo[1][None, :]
    d2 = own_geo[2][:, None] - other_geo[2][None, :]
    dist = d0 * d0 + d1 * d1 + d2 * d2 + EPS2
    proj_own = own_geo[3][:, None] * d0 + own_geo[4][:, None] * d1 + own_geo[5][:, None] * d2
    proj_other = (
        other_geo[3][None, :] * d0 + other_geo[4][None, :] * d1 + other_geo[5][None, :] * d2
    )
    kernel = (
        own_weight[:, None]
        * other_weight[None, :]
        * (proj_own * proj_own + proj_other * proj_other)
        / (dist * dist)
    )
    return jnp.sum(kernel)


def tile(own, other):
    count = own.shape[1]
    rows = count // 2 if count >= 1024 else count

    def visit(index, carry):
        energy, grad_own, grad_other = carry
        start = index * rows
        piece = lax.dynamic_slice_in_dim(own, start, rows, 1)

        def energy_of(first, second):
            return pair_energy(first, piece[6], second, other[6])

        value, pullback = jax.vjp(energy_of, piece[:6], other[:6])
        part_own, part_other = pullback(jnp.ones_like(value))
        grad_own = lax.dynamic_update_slice_in_dim(grad_own, part_own, start, 1)
        return (energy + value, grad_own, grad_other + part_other)

    init = (
        jnp.zeros((), jnp.float32),
        jnp.zeros((6, count), jnp.float32),
        jnp.zeros((6, other.shape[1]), jnp.float32),
    )
    return lax.fori_loop(0, count // rows, visit, init)


def geometry(pos, faces):
    first = pos[:, faces[0]]
    second = pos[:, faces[1]]
    third = pos[:, faces[2]]
    center = (first + second + third) / 3.0
    normal = 0.5 * jnp.cross(second - first, third - first, axis=0)
    return jnp.concatenate([center, normal], 0)


def chain(own, moves, energy, grad):
    moving = own
    carried = jnp.zeros((6, own.shape[1]), jnp.float32)
    for offset in moves:
        moving, carried = from_behind((moving, carried), BLK, offset)
        value, grad_own, grad_other = tile(own, moving)
        energy = energy + value
        grad = grad + grad_own
        carried = carried + grad_other
    carried = from_behind(carried, BLK, -sum(moves))
    return (energy, grad + carried)


def shards(vertices, faces, trial_step, accepted, face_weight, partner_shift):
    count = faces.shape[1]
    pos = vertices + accepted[0].astype(jnp.float32) * trial_step

    def geo_of(p):
        return geometry(p, faces)

    geo, pull = jax.vjp(geo_of, pos)
    own = jnp.concatenate([geo, face_weight[None, :]], 0)
    value, grad_a, grad_b = tile(own, own)
    energy = 0.5 * value
    grad = 0.5 * (grad_a + grad_b)
    energy, grad = chain(own, [-1] * (HOPS // 2), energy, grad)
    energy, grad = chain(own, [HOPS // 2 + 1] + [1] * (HOPS - HOPS // 2 - 1), energy, grad)
    groups = lax.axis_size(GRP)
    blocks = gather_directly(own[None], GRP, 0)
    group = lax.axis_index(GRP)
    rounds = partner_shift.shape[0]
    slots = jnp.zeros((groups, 6, count), jnp.float32)
    for r in range(rounds):
        ahead = (group + partner_shift[r, group]) % groups
        value, grad_own, grad_other = tile(own, lax.dynamic_index_in_dim(blocks, ahead, 0, False))
        energy = energy + value
        grad = grad + grad_own
        chosen = (jnp.arange(groups) == ahead).astype(jnp.float32)
        slots = slots + chosen[:, None, None] * grad_other[None]
    returned = summed_on_arrival(slots, GRP, 0)
    grad = grad + returned[0]
    vertex_grad = pull(grad)[0] / count
    devices = groups * lax.axis_size(BLK)
    total = by_axis(energy, GRP_BLK)
    total = total / (count * count * devices)
    return (vertex_grad, total.reshape(1))


def solution(mesh):
    torus = Mesh(mesh.devices.reshape(2, 2, 8, 4, 4), ("grp_0", "grp_1", "blk_0", "blk_1", "blk_2"))
    placed = (P(None, GRP_BLK), P(None, GRP_BLK), P(None, GRP_BLK), P(GRP), P(GRP_BLK), P())
    return jax.shard_map(
        shards, mesh=torus, in_specs=placed, out_specs=(P(None, GRP_BLK), P()), check_vma=False
    )
```

profile of v0, /device:TPU:10, one launch (start us, length us, event | category | flops | bytes accessed | tf_op | source)
XLA Modules:
  0.0 157.8 jit_solution(12112475461877194847)
XLA Ops:
  0.6 0.8 compare_select_fusion.1
  2.3 1.0 gather_fusion
  3.5 1.0 gather_fusion.1
  4.6 1.0 gather_fusion.2
  6.6 2.4 %collective-permute-start = (f32[7,512]{1,0:T(8,128)S(1)}, f32[7,512]{1,0:T(8,128)S(1)}, u32[]{:S(2)}, u32[]{:S(2)}) collective-permute-start(f32[7,512]{1,0:T(8,128)S(1)} %pad_maximum_fusion), channel_id=1, source_target_pairs={{0,127},{1,0},{2,1},{3,2},{4,3},{5,4},{6,5},{7,6},{8,7},{9,8},{10,... | collective-permute-start | bytes 43016 | tf_op jit(solution)/shard_map/ppermute | solution.py:20
  9.0 6.5 %collective-permute-start.5 = (f32[7,512]{1,0:T(8,128)S(1)}, f32[7,512]{1,0:T(8,128)S(1)}, u32[]{:S(2)}, u32[]{:S(2)}) collective-permute-start(f32[7,512]{1,0:T(8,128)S(1)} %pad_maximum_fusion), channel_id=1, source_target_pairs={{0,3},{1,4},{2,5},{3,6},{4,7},{5,8},{6,9},{7,10},{8,11},{9,12},{10... | collective-permute-start | bytes 43016 | tf_op jit(solution)/shard_map/ppermute | solution.py:20
  15.5 8.5 %collective-permute-start.2 = (f32[6,512]{1,0:T(8,128)S(1)}, f32[6,512]{1,0:T(8,128)S(1)}, u32[]{:S(2)}, u32[]{:S(2)}) collective-permute-start(f32[6,512]{1,0:T(8,128)S(1)} %broadcast.326), channel_id=1, source_target_pairs={{0,127},{1,0},{2,1},{3,2},{4,3},{5,4},{6,5},{7,6},{8,7},{9,8},{10,... | collective-permute-start | bytes 36872 | tf_op jit(solution)/shard_map/ppermute | solution.py:20
  24.0 1.9 %collective-permute-start.7 = (f32[6,512]{1,0:T(8,128)S(1)}, f32[6,512]{1,0:T(8,128)S(1)}, u32[]{:S(2)}, u32[]{:S(2)}) collective-permute-start(f32[6,512]{1,0:T(8,128)S(1)} %broadcast.326), channel_id=1, source_target_pairs={{0,3},{1,4},{2,5},{3,6},{4,7},{5,8},{6,9},{7,10},{8,11},{9,12},{10... | collective-permute-start | bytes 36872 | tf_op jit(solution)/shard_map/ppermute | solution.py:20
  26.6 3.3 %all-to-all-start = ((f32[4,1,7,512]{3,1,2,0:T(1,128)}), f32[4,1,7,512]{3,1,2,0:T(1,128)S(1)}, u32[]{:S(2)}, u32[]{:S(2)}) async-start(f32[4,1,7,512]{3,1,2,0:T(1,128)} %broadcast_in_dim.316), calls=%async_computation | async-start | bytes 114688 | tf_op jit(solution)/shard_map/all_to_all | solution.py:31
  32.5 4.2 %divide_reduce_fusion.5 = (f32[]{:T(128)}, f32[512]{0:T(512)S(1)}, f32[512]{0:T(512)S(1)}, f32[512]{0:T(512)S(1)}, f32[512]{0:T(512)S(1)}, /*index=5*/f32[512]{0...) fusion(f32[512]{0:T(512)S(1)} %bitcast.304, ...), kind=kLoop, calls=%fused_computation.319 | loop fusion | flops 19654656 | bytes 53252 | tf_op jit(solution)/shard_map/while/body/eval_jaxpr/jvp()/reduce_sum | solution.py:70
  36.7 2.7 %collective-permute-start.3 = (f32[6,512]{1,0:T(8,128)S(1)}, f32[6,512]{1,0:T(8,128)S(1)}, u32[]{:S(2)}, u32[]{:S(2)}) collective-permute-start(f32[6,512]{1,0:T(8,128)S(1)} %add_add_fusion.25), channel_id=1, source_target_pairs={{0,127},{1,0},{2,1},{3,2},{4,3},{5,4},{6,5},{7,6},{8,7},{9,8},{10,... | collective-permute-start | bytes 36872 | tf_op jit(solution)/shard_map/ppermute | solution.py:20
  39.5 4.2 %divide_reduce_fusion.3 = (f32[]{:T(128)}, f32[512]{0:T(512)S(1)}, f32[512]{0:T(512)S(1)}, f32[512]{0:T(512)S(1)}, f32[512]{0:T(512)S(1)}, /*index=5*/f32[512]{0...) fusion(f32[512]{0:T(512)S(1)} %bitcast.325, ...), kind=kLoop, calls=%fused_computation.317 | loop fusion | flops 19654656 | bytes 53252 | tf_op jit(solution)/shard_map/while/body/eval_jaxpr/jvp()/reduce_sum | solution.py:70
  43.7 3.4 %collective-permute-start.1 = (f32[7,512]{1,0:T(8,128)S(1)}, f32[7,512]{1,0:T(8,128)S(1)}, u32[]{:S(2)}, u32[]{:S(2)}) collective-permute-start(f32[7,512]{1,0:T(8,128)S(1)} %collective-permute-done), channel_id=1, source_target_pairs={{0,127},{1,0},{2,1},{3,2},{4,3},{5,4},{6,5},{7,6},{8,7},{9,8},{10,... | collective-permute-start | bytes 43016 | tf_op jit(solution)/shard_map/ppermute | solution.py:20
  47.2 2.4 %collective-permute-start.8 = (f32[6,512]{1,0:T(8,128)S(1)}, f32[6,512]{1,0:T(8,128)S(1)}, u32[]{:S(2)}, u32[]{:S(2)}) collective-permute-start(f32[6,512]{1,0:T(8,128)S(1)} %add_add_fusion.23), channel_id=1, source_target_pairs={{0,1},{1,2},{2,3},{3,4},{4,5},{5,6},{6,7},{7,8},{8,9},{9,10},{10,1... | collective-permute-start | bytes 36872 | tf_op jit(solution)/shard_map/ppermute | solution.py:20
  49.6 3.1 %collective-permute-start.6 = (f32[7,512]{1,0:T(8,128)S(1)}, f32[7,512]{1,0:T(8,128)S(1)}, u32[]{:S(2)}, u32[]{:S(2)}) collective-permute-start(f32[7,512]{1,0:T(8,128)S(1)} %collective-permute-done.5), channel_id=1, source_target_pairs={{0,1},{1,2},{2,3},{3,4},{4,5},{5,6},{6,7},{7,8},{8,9},{9,10},{10,1... | collective-permute-start | bytes 43016 | tf_op jit(solution)/shard_map/ppermute | solution.py:20
  52.8 4.2 %divide_reduce_fusion.4 = (f32[]{:T(128)}, f32[512]{0:T(512)S(1)}, f32[512]{0:T(512)S(1)}, f32[512]{0:T(512)S(1)}, f32[512]{0:T(512)S(1)}, /*index=5*/f32[512]{0...) fusion(f32[512]{0:T(512)S(1)} %bitcast.311, ...), kind=kLoop, calls=%fused_computation.318 | loop fusion | flops 19654656 | bytes 53252 | tf_op jit(solution)/shard_map/while/body/eval_jaxpr/jvp()/reduce_sum | solution.py:70
  57.0 7.0 %collective-permute-start.4 = (f32[6,512]{1,0:T(8,128)S(1)}, f32[6,512]{1,0:T(8,128)S(1)}, u32[]{:S(2)}, u32[]{:S(2)}) collective-permute-start(f32[6,512]{1,0:T(8,128)S(1)} %add_add_fusion.24), channel_id=1, source_target_pairs={{0,2},{1,3},{2,4},{3,5},{4,6},{5,7},{6,8},{7,9},{8,10},{9,11},{10,... | collective-permute-start | bytes 36872 | tf_op jit(solution)/shard_map/ppermute | solution.py:20
  64.1 4.2 %divide_reduce_fusion.2 = (f32[]{:T(128)}, f32[512]{0:T(512)S(1)}, f32[512]{0:T(512)S(1)}, f32[512]{0:T(512)S(1)}, f32[512]{0:T(512)S(1)}, /*index=5*/f32[512]{0...) fusion(f32[512]{0:T(512)S(1)} %bitcast.318, ...), kind=kLoop, calls=%fused_computation.316 | loop fusion | flops 19654656 | bytes 53252 | tf_op jit(solution)/shard_map/while/body/eval_jaxpr/jvp()/reduce_sum | solution.py:70
  68.3 4.2 %divide_reduce_fusion.1 = (f32[]{:T(128)}, f32[512]{0:T(512)S(1)}, f32[512]{0:T(512)S(1)}, f32[512]{0:T(512)S(1)}, f32[512]{0:T(512)S(1)}, /*index=5*/f32[512]{0...) fusion(f32[512]{0:T(512)S(1)} %bitcast.348, ...), kind=kLoop, calls=%fused_computation.315 | loop fusion | flops 19654656 | bytes 53252 | tf_op jit(solution)/shard_map/while/body/eval_jaxpr/jvp()/reduce_sum | solution.py:70
  72.6 8.0 %divide_reduce_fusion = (f32[]{:T(128)}, f32[512]{0:T(512)S(1)}, f32[512]{0:T(512)S(1)}, f32[512]{0:T(512)S(1)}, f32[512]{0:T(512)S(1)}, /*index=5*/f32[512]{0:T...) fusion(f32[512]{0:T(512)S(1)} %bitcast.335, ...), kind=kLoop, calls=%fused_computation.314 | loop fusion | flops 39309312 | bytes 77832 | tf_op jit(solution)/shard_map/while/body/eval_jaxpr/jvp()/reduce_sum | solution.py:70
  80.7 0.7 multiply_add_fusion
  81.4 3.3 %all-to-all-start.1 = ((f32[4,1,6,512]{3,1,2,0:T(1,128)}), f32[4,1,6,512]{3,1,2,0:T(1,128)S(1)}, u32[]{:S(2)}, u32[]{:S(2)}) async-start(f32[4,1,6,512]{3,1,2,0:T(1,128)} %multiply_add_fusion), calls=%async_computation.1 | async-start | bytes 98304 | tf_op jit(solution)/shard_map/all_to_all | solution.py:47
  84.7 7.9 %collective-permute-start.9 = (f32[6,512]{1,0:T(8,128)S(1)}, f32[6,512]{1,0:T(8,128)S(1)}, u32[]{:S(2)}, u32[]{:S(2)}) collective-permute-start(f32[6,512]{1,0:T(8,128)S(1)} %add_add_fusion.22), channel_id=1, source_target_pairs={{0,124},{1,125},{2,126},{3,127},{4,0},{5,1},{6,2},{7,3},{8,4},{9,5... | collective-permute-start | bytes 36872 | tf_op jit(solution)/shard_map/ppermute | solution.py:20
  97.0 5.4 %psum.35 = f32[]{:T(128)} all-reduce(f32[]{:T(128)S(6)} %add.724), channel_id=1, replica_groups=mesh['grp_0'=2,'grp_1'=2,'blk_0'=8,'blk_1'=4,'blk_2'=4] {'grp_0'}, use_global_device_ids=true, to_apply=%region_95.0 | all-reduce | flops 1 | bytes 8 | tf_op jit(solution)/shard_map/psum | solution.py:52
  102.4 3.1 %psum.36 = f32[]{:T(128)} all-reduce(f32[]{:T(128)} %psum.35), channel_id=1, replica_groups=mesh['grp_0'=2,'grp_1'=2,'blk_0'=8,'blk_1'=4,'blk_2'=4] {'grp_1'}, use_global_device_ids=true, to_apply=%region_96.0 | all-reduce | flops 1 | bytes 8 | tf_op jit(solution)/shard_map/psum | solution.py:52
  105.5 20.6 %psum.37 = f32[]{:T(128)} all-reduce(f32[]{:T(128)} %psum.36), channel_id=1, replica_groups=mesh['grp_0'=2,'grp_1'=2,'blk_0'=8,'blk_1'=4,'blk_2'=4] {'blk_0'}, use_global_device_ids=true, to_apply=%region_97.0 | all-reduce | flops 1 | bytes 8 | tf_op jit(solution)/shard_map/psum | solution.py:52
  126.1 9.2 %psum.38 = f32[]{:T(128)} all-reduce(f32[]{:T(128)} %psum.37), channel_id=1, replica_groups=mesh['grp_0'=2,'grp_1'=2,'blk_0'=8,'blk_1'=4,'blk_2'=4] {'blk_1'}, use_global_device_ids=true, to_apply=%region_98.0 | all-reduce | flops 1 | bytes 8 | tf_op jit(solution)/shard_map/psum | solution.py:52
  135.4 11.1 %psum.39 = f32[]{:T(128)} all-reduce(f32[]{:T(128)} %psum.38), channel_id=1, replica_groups=mesh['grp_0'=2,'grp_1'=2,'blk_0'=8,'blk_1'=4,'blk_2'=4] {'blk_2'}, use_global_device_ids=true, to_apply=%region_99.0 | all-reduce | flops 1 | bytes 8 | tf_op jit(solution)/shard_map/psum | solution.py:52
  147.7 2.3 %scatter_custom_fusion.1 = f32[3,256]{0,1:T(8,128)S(1)} fusion(s32[512]{0:T(512)S(1)} %bitcast.254, f32[512,3]{1,0:T(8,128)S(1)} %copy.416, f32[]{:T(128)} %constant.115.clone.1), kind=kCustom, calls=%fused_computation.335 | custom fusion | flops 1536 | bytes 3076 | tf_op jit(solution)/shard_map/transpose(jvp())/scatter-add | solution.py:100
  150.1 2.3 %scatter_custom_fusion = f32[3,256]{0,1:T(8,128)S(1)} fusion(s32[512]{0:T(512)S(1)} %bitcast.252, f32[512,3]{1,0:T(8,128)S(1)} %copy.415, f32[]{:T(128)} %constant.115.clone.1), kind=kCustom, calls=%fused_computation.337 | custom fusion | flops 1536 | bytes 3076 | tf_op jit(solution)/shard_map/transpose(jvp())/scatter-add | solution.py:101
  152.6 3.4 %scatter_fusion = f32[3,256]{0,1:T(8,128)S(1)} fusion(f32[3,256]{0,1:T(8,128)S(1)} %add_any.844, s32[512]{0:T(512)S(1)} %bitcast.229, f32[512,3]{1,0:T(8,128)S(1)} %copy.417), kind=kCustom, calls=%fused_computation.5 | custom fusion | flops 1536 | bytes 20480 | tf_op jit(solution)/shard_map/transpose(jvp())/scatter-add | solution.py:99
  156.0 0.7 copy.418
  (80 shorter events, 4.2 us)
Async XLA Ops:
  1.5 0.7 copy-start.1
  1.5 0.7 copy-start
  5.9 0.7 copy-start.2
  6.6 25.9 %collective-permute-start = (f32[7,512]{1,0:T(8,128)S(1)}, f32[7,512]{1,0:T(8,128)S(1)}, u32[]{:S(2)}, u32[]{:S(2)}) collective-permute-start(f32[7,512]{1,0:T(8,128)S(1)} %pad_maximum_fusion), channel_id=1, source_target_pairs={{0,127},{1,0},{2,1},{3,2},{4,3},{5,4},{6,5},{7,6},{8,7},{9,8},{10,... | collective-permute-start | bytes 43016 | tf_op jit(solution)/shard_map/ppermute | solution.py:20
  9.0 30.5 %collective-permute-start.5 = (f32[7,512]{1,0:T(8,128)S(1)}, f32[7,512]{1,0:T(8,128)S(1)}, u32[]{:S(2)}, u32[]{:S(2)}) collective-permute-start(f32[7,512]{1,0:T(8,128)S(1)} %pad_maximum_fusion), channel_id=1, source_target_pairs={{0,3},{1,4},{2,5},{3,6},{4,7},{5,8},{6,9},{7,10},{8,11},{9,12},{10... | collective-permute-start | bytes 43016 | tf_op jit(solution)/shard_map/ppermute | solution.py:20
  15.5 21.2 %collective-permute-start.2 = (f32[6,512]{1,0:T(8,128)S(1)}, f32[6,512]{1,0:T(8,128)S(1)}, u32[]{:S(2)}, u32[]{:S(2)}) collective-permute-start(f32[6,512]{1,0:T(8,128)S(1)} %broadcast.326), channel_id=1, source_target_pairs={{0,127},{1,0},{2,1},{3,2},{4,3},{5,4},{6,5},{7,6},{8,7},{9,8},{10,... | collective-permute-start | bytes 36872 | tf_op jit(solution)/shard_map/ppermute | solution.py:20
  24.0 23.2 %collective-permute-start.7 = (f32[6,512]{1,0:T(8,128)S(1)}, f32[6,512]{1,0:T(8,128)S(1)}, u32[]{:S(2)}, u32[]{:S(2)}) collective-permute-start(f32[6,512]{1,0:T(8,128)S(1)} %broadcast.326), channel_id=1, source_target_pairs={{0,3},{1,4},{2,5},{3,6},{4,7},{5,8},{6,9},{7,10},{8,11},{9,12},{10... | collective-permute-start | bytes 36872 | tf_op jit(solution)/shard_map/ppermute | solution.py:20
  26.6 41.7 %all-to-all-start = ((f32[4,1,7,512]{3,1,2,0:T(1,128)}), f32[4,1,7,512]{3,1,2,0:T(1,128)S(1)}, u32[]{:S(2)}, u32[]{:S(2)}) async-start(f32[4,1,7,512]{3,1,2,0:T(1,128)} %broadcast_in_dim.316), calls=%async_computation | async-start | bytes 114688 | tf_op jit(solution)/shard_map/all_to_all | solution.py:31
  29.9 0.7 copy-start.3
  36.7 20.3 %collective-permute-start.3 = (f32[6,512]{1,0:T(8,128)S(1)}, f32[6,512]{1,0:T(8,128)S(1)}, u32[]{:S(2)}, u32[]{:S(2)}) collective-permute-start(f32[6,512]{1,0:T(8,128)S(1)} %add_add_fusion.25), channel_id=1, source_target_pairs={{0,127},{1,0},{2,1},{3,2},{4,3},{5,4},{6,5},{7,6},{8,7},{9,8},{10,... | collective-permute-start | bytes 36872 | tf_op jit(solution)/shard_map/ppermute | solution.py:20
  43.7 9.0 %collective-permute-start.1 = (f32[7,512]{1,0:T(8,128)S(1)}, f32[7,512]{1,0:T(8,128)S(1)}, u32[]{:S(2)}, u32[]{:S(2)}) collective-permute-start(f32[7,512]{1,0:T(8,128)S(1)} %collective-permute-done), channel_id=1, source_target_pairs={{0,127},{1,0},{2,1},{3,2},{4,3},{5,4},{6,5},{7,6},{8,7},{9,8},{10,... | collective-permute-start | bytes 43016 | tf_op jit(solution)/shard_map/ppermute | solution.py:20
  47.2 37.5 %collective-permute-start.8 = (f32[6,512]{1,0:T(8,128)S(1)}, f32[6,512]{1,0:T(8,128)S(1)}, u32[]{:S(2)}, u32[]{:S(2)}) collective-permute-start(f32[6,512]{1,0:T(8,128)S(1)} %add_add_fusion.23), channel_id=1, source_target_pairs={{0,1},{1,2},{2,3},{3,4},{4,5},{5,6},{6,7},{7,8},{8,9},{9,10},{10,1... | collective-permute-start | bytes 36872 | tf_op jit(solution)/shard_map/ppermute | solution.py:20
  49.6 14.5 %collective-permute-start.6 = (f32[7,512]{1,0:T(8,128)S(1)}, f32[7,512]{1,0:T(8,128)S(1)}, u32[]{:S(2)}, u32[]{:S(2)}) collective-permute-start(f32[7,512]{1,0:T(8,128)S(1)} %collective-permute-done.5), channel_id=1, source_target_pairs={{0,1},{1,2},{2,3},{3,4},{4,5},{5,6},{6,7},{7,8},{8,9},{9,10},{10,1... | collective-permute-start | bytes 43016 | tf_op jit(solution)/shard_map/ppermute | solution.py:20
  57.0 90.2 %collective-permute-start.4 = (f32[6,512]{1,0:T(8,128)S(1)}, f32[6,512]{1,0:T(8,128)S(1)}, u32[]{:S(2)}, u32[]{:S(2)}) collective-permute-start(f32[6,512]{1,0:T(8,128)S(1)} %add_add_fusion.24), channel_id=1, source_target_pairs={{0,2},{1,3},{2,4},{3,5},{4,6},{5,7},{6,8},{7,9},{8,10},{9,11},{10,... | collective-permute-start | bytes 36872 | tf_op jit(solution)/shard_map/ppermute | solution.py:20
  81.4 65.8 %all-to-all-start.1 = ((f32[4,1,6,512]{3,1,2,0:T(1,128)}), f32[4,1,6,512]{3,1,2,0:T(1,128)S(1)}, u32[]{:S(2)}, u32[]{:S(2)}) async-start(f32[4,1,6,512]{3,1,2,0:T(1,128)} %multiply_add_fusion), calls=%async_computation.1 | async-start | bytes 98304 | tf_op jit(solution)/shard_map/all_to_all | solution.py:47
  84.7 62.5 %collective-permute-start.9 = (f32[6,512]{1,0:T(8,128)S(1)}, f32[6,512]{1,0:T(8,128)S(1)}, u32[]{:S(2)}, u32[]{:S(2)}) collective-permute-start(f32[6,512]{1,0:T(8,128)S(1)} %add_add_fusion.22), channel_id=1, source_target_pairs={{0,124},{1,125},{2,126},{3,127},{4,0},{5,1},{6,2},{7,3},{8,4},{9,5... | collective-permute-start | bytes 36872 | tf_op jit(solution)/shard_map/ppermute | solution.py:20
where the time goes:
time: 159 us; the launch traced here: 158 us
  starting transfers between devices  52.4 us (33%)
  blocking collectives  49.5 us (31%)
  other arithmetic  39.1 us (25%)
  between operations  9.32 us (6%)
  local copies, waits for them, and re-layouts  7.39 us (5%)
    psum x5, blocking collectives, by_axis(): return functools.reduce(lax.psum, axes, value)  49.5 us
    ppermute x10, starting transfers between devices, from_behind(): lax.ppermute(value, axis, [(i, (i + by) % count) for i in range(count)])  45.8 us
    reduce_sum x6, other arithmetic, pair_energy(): return jnp.sum(kernel)  29.1 us
    scatter-add x1, other arithmetic, geometry(): first = pos[:, faces[0]]  3.37 us
    all_to_all x1, starting transfers between devices, summed_on_arrival(): parts = lax.all_to_all(in_blocks(value, dim, count), axis, 0, 0, tiled=True)  3.28 us
    all_to_all x1, starting transfers between devices, from_everyone(): lax.all_to_all(jnp.broadcast_to(value[None], (count, *value.shape)), axis...  3.28 us
  transfers between devices with their start and end apart: 12, of which 0 were waited for; matrix products, arithmetic and copies ran while one was open for 20% of the time, Pallas kernels for 0%

commit v1 on v0

v1 whole, which is shorter than its diff:
```python
import functools

import jax
import jax.numpy as jnp
from jax import lax
from jax.experimental import pallas as pl
from jax.experimental.pallas import tpu as pltpu
from jax.sharding import PartitionSpec as P

F = jnp.float32
B = jnp.bfloat16
EPS2 = 0.05
HOPS = 4
CHUNK = 128
LANES = 256
ROWS = 16
MESH = pl.DeviceIdType.MESH

TILES = (
    [("grp", 2), ("grp", 1)]
    + [("blk", k) for k in range(1, HOPS + 1)]
    + [("grp", 3)]
    + [("blk", -k) for k in range(1, HOPS + 1)]
)
HALF_AT = 2
FULL_AT = 7
Y, ZH, X, G = 8, 4, 4, 4


def split3(x):
    h = x.astype(B).astype(F)
    r = x - h
    m = r.astype(B).astype(F)
    return h, m, r - m


def dot(a, b):
    return jnp.dot(a, b, preferred_element_type=F)


def cross(a, b):
    return [
        a[1] * b[2] - a[2] * b[1],
        a[2] * b[0] - a[0] * b[2],
        a[0] * b[1] - a[1] * b[0],
    ]


def rows_of(x, n=3):
    return [x[k : k + 1] for k in range(n)]


def own_prep(own, ra, rb, cj):
    n = own.shape[1]
    z = jnp.zeros((1, n), F)
    ya = jnp.concatenate([-own[3:6], z, z, z, own[7:8], z], 0)
    yb = jnp.concatenate([z, z, z, own[0:3], z, z - 1.0], 0)
    for y, r in ((ya, ra), (yb, rb)):
        h, m, low = split3(y)
        r[...] = jnp.concatenate([h, m, low, h, m, h], 0).astype(B)
    for k in range(3):
        cj[k] = jnp.broadcast_to(own[k : k + 1], (8, n))


def other_prep(blk, wrow, xt, ct, fs):
    row = lax.broadcasted_iota(jnp.int32, blk.shape, 0)
    x = jnp.where(row == 6, 1.0, blk)
    h, m, low = split3(x)
    tr = jnp.concatenate([h, h, h, m, m, low, blk, blk], 0).T
    xt[...] = tr[:, :48].astype(B)
    ct[...] = tr[:, 48:56]
    h, m, low = split3(x * wrow)
    fs[...] = jnp.concatenate([h, m, low, jnp.zeros_like(low)], 0).astype(B)


def pairs(ct, cj, ab, co, slot, base, r0):
    n = cj.shape[2]
    rows = slice(base + r0, base + r0 + ROWS)
    cr = slice(r0, r0 + ROWS)
    for l0 in range(0, n, LANES):
        ls = slice(l0, l0 + LANES)
        d = []
        for k in range(3):
            other = jnp.broadcast_to(ct[rows, k : k + 1], (ROWS, LANES))
            own = cj[k, :, ls]
            d.append(jnp.concatenate([own] * (ROWS // 8), 0) - other)
        q = 1.0 / ((d[0] * d[0] + EPS2) + (d[1] * d[1] + d[2] * d[2]))
        q2 = q * q
        a = ab[slot, 0, cr, ls]
        b = ab[slot, 1, cr, ls]
        al = a * q2
        be = b * q2
        ga = (a * al + b * be) * q
        for m, v in enumerate((al, be, ga)):
            h = v.astype(B)
            co[slot, 2 * m, cr, ls] = h
            co[slot, 2 * m + 1, cr, ls] = (v - h.astype(F)).astype(B)


def tile(xt, ct, fs, ra, rb, cj, ab, co, acc):
    chunks = cj.shape[2] // CHUNK

    def project(c):
        x = xt[c * CHUNK : (c + 1) * CHUNK, :]
        ab[c % 2, 0] = dot(x, ra[...])
        ab[c % 2, 1] = dot(x, rb[...])

    project(0)
    for c in range(chunks):
        if c + 1 < chunks:
            project(c + 1)
        for r0 in range(0, CHUNK, ROWS):
            pairs(ct, cj, ab, co, c % 2, c * CHUNK, r0)
        f = fs[:, c * CHUNK : (c + 1) * CHUNK]
        for m in range(3):
            acc[m] += dot(f, co[c % 2, 2 * m]) + dot(f, co[c % 2, 2 * m + 1])


def sums_of(acc):
    return [acc[m, 0:8, :] + acc[m, 8:16, :] + acc[m, 16:24, :] for m in range(3)]


def grad_normal(own, s):
    return own[0:3] * s[0][6:7] - s[0][0:3]


def energy_of(own, acc):
    s = sums_of(acc)
    e = jnp.sum(own[3:6] * grad_normal(own, s) + own[0:3] * s[1][3:6], 0, keepdims=True)
    e = (e - s[1][7:8]) * own[6:7]
    n = e.shape[1]
    return functools.reduce(jnp.add, [e[:, k : k + 128] for k in range(0, n, 128)])


def kernel(
    ver_ref, faces_ref, step_ref, weight_ref, acc_ref, shift_ref, grad_ref, energy_ref,
    blocks, hot, xt, ct, fs, ra, rb, cj, ab, co, acc, part,
    box_a, box_b, box_c, send, recv, send_a, recv_a, send_b, recv_b, send_c, recv_c,
):
    g = lax.axis_index("grp")
    b = lax.axis_index("blk")
    blk_n = Y * ZH * X
    y, zh, x = b // (ZH * X), (b // X) % ZH, b % X

    def peer_a(i):
        j = (g * ZH + zh + i) % (G * ZH)
        return (j // ZH, (y * ZH + j % ZH) * X + x)

    def peer_b(i):
        return (g, (((y + i) % Y) * ZH + zh) * X + x)

    def peer_c(i):
        return (g, (y * ZH + zh) * X + (x + i) % X)

    def visitor(axis, k):
        if axis == "grp":
            return ((g + G - k) % G, b)
        return (g, (b + blk_n - k) % blk_n)

    peers = [visitor(*t) for t in TILES if t[0] == "blk"]
    peers += [peer_a(i) for i in range(1, G * ZH)]
    peers += [peer_b(i) for i in range(1, Y)] + [peer_c(i) for i in range(1, X)]
    barrier = pltpu.get_barrier_semaphore()
    for p in peers:
        pl.semaphore_signal(barrier, inc=1, device_id=p, device_id_type=MESH)

    verts, count = ver_ref.shape[1], faces_ref.shape[1]
    pos = ver_ref[...] + acc_ref[0].astype(F) * step_ref[...]
    table = jnp.concatenate([*split3(pos), jnp.zeros((7, verts), F)], 0).astype(B)
    vert = lax.broadcasted_iota(jnp.int32, (verts, count), 0)
    corners = []
    for k in range(3):
        hot[k] = jnp.where(vert == faces_ref[k : k + 1, :], 1.0, 0.0).astype(B)
        u = dot(table, hot[k])
        corners.append(u[0:3] + u[3:6] + u[6:9])
    center = (corners[0] + corners[1] + corners[2]) / 3.0
    e1 = rows_of(corners[1] - corners[0])
    e2 = rows_of(corners[2] - corners[0])
    normal = 0.5 * jnp.concatenate(cross(e1, e2), 0)
    offset = jnp.sum(center * normal, 0, keepdims=True)
    own = jnp.concatenate([center, normal, weight_ref[...], offset], 0)
    blocks[0] = own

    pl.semaphore_wait(barrier, len(peers))

    def block_copy(t, to):
        return pltpu.make_async_remote_copy(
            src_ref=blocks.at[0], dst_ref=blocks.at[t], send_sem=send.at[t - 1],
            recv_sem=recv.at[t - 1], device_id=to, device_id_type=MESH,
        )

    for t, where in enumerate(TILES):
        block_copy(t + 1, visitor(*where)).start()

    own_prep(own, ra, rb, cj)
    acc[...] = jnp.zeros_like(acc)

    def times(k):
        total = jnp.float32(0.0)
        for r in range(shift_ref.shape[0]):
            total += jnp.where(shift_ref[r, g] == k, 1.0, 0.0)
            total += jnp.where(shift_ref[r, (g + k) % G] == G - k, 1.0, 0.0)
        return total

    times_of = {k: times(k) for k in range(1, G)}

    def spread(value, box, send_sem, recv_sem, peer, n):
        box[0] = value
        for i in range(1, n):
            pltpu.make_async_remote_copy(
                src_ref=box.at[0], dst_ref=box.at[i], send_sem=send_sem.at[i - 1],
                recv_sem=recv_sem.at[i - 1], device_id=peer(i), device_id_type=MESH,
            ).start()

    def gathered(box, send_sem, recv_sem, peer, n):
        for i in range(1, n):
            pltpu.make_async_remote_copy(
                src_ref=box.at[0], dst_ref=box.at[i], send_sem=send_sem.at[i - 1],
                recv_sem=recv_sem.at[i - 1], device_id=peer(i), device_id_type=MESH,
            ).wait()
        return functools.reduce(jnp.add, [box[i] for i in range(n)])

    boxes = (
        (box_a, send_a, recv_a, peer_a, G * ZH),
        (box_b, send_b, recv_b, peer_b, Y),
        (box_c, send_c, recv_c, peer_c, X),
    )

    def visit(t, carry):
        @pl.when(t > 0)
        def _():
            block_copy(t, visitor("blk", 1)).wait_recv()

        @pl.when(t == HALF_AT)
        def _():
            part[...] = energy_of(own, acc)

        @pl.when(t == FULL_AT)
        def _():
            spread(energy_of(own, acc) - 0.5 * part[...], *boxes[0])

        @pl.when(t == FULL_AT + 2)
        def _():
            spread(gathered(*boxes[0]), *boxes[1])

        @pl.when(t == FULL_AT + 4)
        def _():
            spread(gathered(*boxes[1]), *boxes[2])

        blk = blocks[t]
        scale = jnp.float32(1.0)
        for i, (axis, k) in enumerate(TILES):
            if axis == "grp":
                scale = jnp.where(t == i + 1, times_of[k], scale)
        other_prep(blk, blk[6:7] * scale, xt, ct, fs)
        tile(xt, ct, fs, ra, rb, cj, ab, co, acc)
        return carry

    lax.fori_loop(0, len(TILES) + 1, visit, 0)

    s = sums_of(acc)
    twice = 2.0 * own[6:7]
    gn = rows_of(grad_normal(own, s) * twice)
    gc = own[3:6] * s[0][6:7] + s[1][3:6] - 2.0 * (own[0:3] * s[2][6:7] - s[2][0:3])
    gc = gc * (twice / 3.0)
    g1 = 0.5 * jnp.concatenate(cross(e2, gn), 0)
    g2 = 0.5 * jnp.concatenate(cross(gn, e1), 0)
    total = jnp.zeros((16, verts), F)
    for k, gu in enumerate((gc - g1 - g2, gc + g1, gc + g2)):
        parts = jnp.concatenate([*split3(gu), jnp.zeros((7, count), F)], 0).astype(B)
        total += lax.dot_general(parts, hot[k], (((1,), (1,)), ((), ())), preferred_element_type=F)
    grad_ref[...] = (total[0:3] + total[3:6] + total[6:9]) * (1.0 / count)

    for t, where in enumerate(TILES):
        block_copy(t + 1, visitor(*where)).wait_send()
    energy_ref[0] = jnp.sum(gathered(*boxes[2])) * (1.0 / (count * count * G * blk_n))


def shards(vertices, faces, trial_step, accepted, face_weight, partner_shift):
    verts, count = vertices.shape[1], faces.shape[1]
    vmem = pl.BlockSpec(memory_space=pltpu.VMEM)
    smem = pl.BlockSpec(memory_space=pltpu.SMEM)
    dma = pltpu.SemaphoreType.DMA
    n = len(TILES)
    return tuple(pl.pallas_call(
        kernel,
        out_shape=(jax.ShapeDtypeStruct((3, verts), F), jax.ShapeDtypeStruct((1,), F)),
        in_specs=[vmem] * 4 + [smem] * 2,
        out_specs=(vmem, smem),
        scratch_shapes=[
            pltpu.VMEM((n + 1, 8, count), F),
            pltpu.VMEM((3, verts, count), B),
            pltpu.VMEM((count, 48), B),
            pltpu.VMEM((count, 8), F),
            pltpu.VMEM((32, count), B),
            pltpu.VMEM((48, count), B),
            pltpu.VMEM((48, count), B),
            pltpu.VMEM((3, 8, count), F),
            pltpu.VMEM((2, 2, CHUNK, count), F),
            pltpu.VMEM((2, 6, CHUNK, count), B),
            pltpu.VMEM((3, 32, count), F),
            pltpu.VMEM((1, 128), F),
            pltpu.VMEM((G * ZH, 1, 128), F),
            pltpu.VMEM((Y, 1, 128), F),
            pltpu.VMEM((X, 1, 128), F),
            dma((n,)), dma((n,)),
            dma((G * ZH - 1,)), dma((G * ZH - 1,)),
            dma((Y - 1,)), dma((Y - 1,)),
            dma((X - 1,)), dma((X - 1,)),
        ],
        compiler_params=pltpu.CompilerParams(collective_id=0, has_side_effects=True),
    )(vertices, faces, trial_step, face_weight.reshape(1, count), accepted, partner_shift))


def solution(mesh):
    both = ("grp", "blk")
    placed = (P(None, both), P(None, both), P(None, both), P("grp"), P(both), P())
    return jax.shard_map(
        shards, mesh=mesh, in_specs=placed, out_specs=(P(None, both), P()), check_vma=False
    )
```

time: 159 us -> 45.1 us (0.28)
  the two profiles are of different devices: /device:TPU:10 before, /device:TPU:1 now
where the time goes in v1:
time: 45.1 us; the launch traced here: 44.7 us
  Pallas kernels  40.4 us (90%)
  between operations  3.05 us (7%)
  local copies, waits for them, and re-layouts  1.27 us (3%)
    pallas_call x1, Pallas kernels, shards(): pl.pallas_call(kernel, out_shape=(jax.ShapeDtypeStruct((3, verts), F), ja...  40.4 us
    unnamed x1, local copies, waits for them, and re-layouts  1.27 us

profile of v1, /device:TPU:1, one launch (start us, length us, event | category | flops | bytes accessed | tf_op | source)
XLA Modules:
  0.0 44.7 jit_solution(8646781953396112069)
XLA Ops:
  1.3 40.4 %shard_map.77 = (f32[3,256]{1,0:T(4,128)}, f32[1]{0:T(128)}) custom-call(f32[3,256]{1,0:T(4,128)} %ver_ref.1, s32[3,512]{1,0:T(4,128)} %faces_ref.1, f32[3,256]{1,0:T(4,128)} %step_ref.1, f32[1,512]{1,0:T(1,128)} %bitcast.1, s32[1]{0:T(128)S(6)} %copy.10.acc_ref, s32[2,4]{1,0:T(2,128)} %shift_ref.1), custom_call_target="tpu_custom_call" | custom-call | tf_op jit(solution)/shard_map/pallas_call | solution.py:285
  41.7 1.3 %copy.11 = f32[3,256]{1,0:T(4,128)} copy(f32[3,256]{1,0:T(4,128)} %get-tuple-element.4) | data formatting | bytes 6144

commit v2 on v1

v2 whole, which is shorter than its diff:
```python
import functools

import jax
import jax.numpy as jnp
from jax import lax
from jax.experimental import pallas as pl
from jax.experimental.pallas import tpu as pltpu
from jax.sharding import PartitionSpec as P

F = jnp.float32
B = jnp.bfloat16
EPS2 = 0.05
HOPS = 4
CHUNK = 256
LANES = 256
ROWS = 16
MESH = pl.DeviceIdType.MESH
Y, ZH, X, G = 8, 4, 4, 4

TILES = (
    [("grp", 2), ("grp", 3)]
    + [("blk", -k) for k in range(1, HOPS + 1)]
    + [("grp", 1)]
    + [("blk", k) for k in range(1, HOPS + 1)]
)
SAVED = 7
COUNT = len(TILES) + 1


def split3(x):
    h = x.astype(B).astype(F)
    r = x - h
    m = r.astype(B).astype(F)
    return h, m, r - m


def dot(a, b):
    return jnp.dot(a, b, preferred_element_type=F)


def cross(a, b):
    return [
        a[1] * b[2] - a[2] * b[1],
        a[2] * b[0] - a[0] * b[2],
        a[0] * b[1] - a[1] * b[0],
    ]


def rows_of(x, n=3):
    return [x[k : k + 1] for k in range(n)]


def own_prep(own, root, ra, rb, cj):
    n = own.shape[1]
    z = jnp.zeros((1, n), F)
    ya = jnp.concatenate([-own[3:6], z, z, z, own[7:8], z], 0)
    yb = jnp.concatenate([z, z, z, own[0:3], z, z - 1.0], 0)
    for y, r in ((ya, ra), (yb, rb)):
        h, m, low = split3(y * root)
        r[...] = jnp.concatenate([h, m, low, h, m, h], 0).astype(B)
    for k in range(3):
        cj[k] = jnp.broadcast_to(own[k : k + 1], (8, n))


def prepare(blk, scale, xt, ct, fs, t):
    row = lax.broadcasted_iota(jnp.int32, blk.shape, 0)
    x = jnp.where(row == 6, 1.0, blk)
    h, m, low = split3(x * jnp.sqrt(blk[6:7] * scale))
    tr = jnp.concatenate([h, h, h, m, m, low, blk, blk], 0).T
    xt[...] = tr[:, :48].astype(B)
    ct[...] = tr[:, 48:56]
    z = jnp.zeros_like(x)
    fs[t] = jnp.concatenate([h, m, low, z, *split3(x), z], 0).astype(B)


def inverse(ct, cj, rows, ls):
    d = []
    for k in range(3):
        other = jnp.broadcast_to(ct[rows, k : k + 1], (ROWS, LANES))
        own = cj[k, :, ls]
        d.append(jnp.concatenate([own] * (ROWS // 8), 0) - other)
    return 1.0 / ((d[0] * d[0] + EPS2) + (d[1] * d[1] + d[2] * d[2]))


def slabs(first, rows, lanes):
    for r0 in range(first, first + rows, ROWS):
        for l0 in range(0, lanes, LANES):
            yield slice(r0, r0 + ROWS), slice(l0, l0 + LANES)


def energy_pass(ct, cj, ab, i, qk, t, eacc):
    n = cj.shape[2]
    e = [eacc[:, k : k + 128] for k in range(0, n, 128)]
    for rows, ls in slabs(0, n, n):
        q = inverse(ct, cj, rows, ls)
        a = ab[i, 0, rows, ls]
        b = ab[i, 1, rows, ls]
        kern = (a * a + b * b) * (q * q)
        qk[t, 0, rows, ls] = q
        qk[t, 1, rows, ls] = kern
        for k in range(0, LANES, 128):
            for r in range(0, ROWS, 8):
                e[(ls.start + k) // 128] += kern[r : r + 8, k : k + 128]
    for k, v in enumerate(e):
        eacc[:, k * 128 : (k + 1) * 128] = v


def store_parts(co, c, cr, ls, values):
    for m, v in enumerate(values):
        h = v.astype(B)
        co[c, 2 * m, cr, ls] = h
        co[c, 2 * m + 1, cr, ls] = (v - h.astype(F)).astype(B)


def reduce_chunk(co, c, fs, t, acc):
    ks = slice(c * CHUNK, (c + 1) * CHUNK)
    for m in range(3):
        first = 32 if m == 2 else 0
        f = fs[t, first : first + 32, ks]
        acc[m] += dot(f, co[c, 2 * m]) + dot(f, co[c, 2 * m + 1])


def grad_pass(values, co, fs, t, before, acc, n):
    chunks = n // CHUNK
    for c in range(chunks):
        for rows, ls in slabs(c * CHUNK, CHUNK, n):
            cr = slice(rows.start - c * CHUNK, rows.stop - c * CHUNK)
            store_parts(co, c, cr, ls, values(rows, ls))
        if c == 0:
            reduce_chunk(co, chunks - 1, fs, before, acc)
        else:
            reduce_chunk(co, c - 1, fs, t, acc)


def saved_values(ab, i, qk, t):
    def values(rows, ls):
        q = qk[t, 0, rows, ls]
        q2 = q * q
        return ab[i, 0, rows, ls] * q2, ab[i, 1, rows, ls] * q2, qk[t, 1, rows, ls] * q

    return values


def full_values(ct, cj, ab, i):
    def values(rows, ls):
        q = inverse(ct, cj, rows, ls)
        q2 = q * q
        a = ab[i, 0, rows, ls]
        b = ab[i, 1, rows, ls]
        al = a * q2
        be = b * q2
        return al, be, (a * al + b * be) * q

    return values


def kernel(
    ver_hbm, faces_hbm, step_hbm, weight_hbm, acc_hbm, shift_hbm, grad_ref, energy_ref,
    ver_ref, faces_ref, step_ref, weight_ref, acc_ref, shift_ref, in_sem,
    blocks, hot, xt0, xt1, ct0, ct1, fs, ra, rb, cj, ab0, ab1, qk, co, acc, eacc,
    box_a, box_b, box_c, send, recv, send_a, recv_a, send_b, recv_b, send_c, recv_c,
):
    g = lax.axis_index("grp")
    b = lax.axis_index("blk")
    blk_n = Y * ZH * X
    y, zh, x = b // (ZH * X), (b // X) % ZH, b % X

    def peer_a(i):
        j = (g * ZH + zh + i) % (G * ZH)
        return (j // ZH, (y * ZH + j % ZH) * X + x)

    def peer_b(i):
        return (g, (((y + i) % Y) * ZH + zh) * X + x)

    def peer_c(i):
        return (g, (y * ZH + zh) * X + (x + i) % X)

    def visitor(axis, k):
        if axis == "grp":
            return ((g + G - k) % G, b)
        return (g, (b + blk_n - k) % blk_n)

    peers = [visitor(*t) for t in TILES if t[0] == "blk"]
    peers += [peer_a(i) for i in range(1, G * ZH)]
    peers += [peer_b(i) for i in range(1, Y)] + [peer_c(i) for i in range(1, X)]
    barrier = pltpu.get_barrier_semaphore()
    for p in peers:
        pl.semaphore_signal(barrier, inc=1, device_id=p, device_id_type=MESH)

    loads = [
        pltpu.make_async_copy(src, dst, in_sem.at[i])
        for i, (src, dst) in enumerate((
            (ver_hbm, ver_ref), (step_hbm, step_ref), (faces_hbm, faces_ref),
            (weight_hbm, weight_ref), (acc_hbm, acc_ref), (shift_hbm, shift_ref),
        ))
    ]
    for c in loads:
        c.start()
    acc[...] = jnp.zeros_like(acc)
    eacc[...] = jnp.zeros_like(eacc)
    co[co.shape[0] - 1] = jnp.zeros(co.shape[1:], B)
    for c in loads:
        c.wait()

    verts, count = ver_ref.shape[1], faces_ref.shape[1]
    pos = ver_ref[...] + acc_ref[0].astype(F) * step_ref[...]
    table = jnp.concatenate([*split3(pos), jnp.zeros((7, verts), F)], 0).astype(B)
    vert = lax.broadcasted_iota(jnp.int32, (verts, count), 0)
    corners = []
    for k in range(3):
        hot[k] = jnp.where(vert == faces_ref[k : k + 1, :], 1.0, 0.0).astype(B)
        u = dot(table, hot[k])
        corners.append(u[0:3] + u[3:6] + u[6:9])
    center = (corners[0] + corners[1] + corners[2]) / 3.0
    e1 = rows_of(corners[1] - corners[0])
    e2 = rows_of(corners[2] - corners[0])
    normal = 0.5 * jnp.concatenate(cross(e1, e2), 0)
    offset = jnp.sum(center * normal, 0, keepdims=True)
    own = jnp.concatenate([center, normal, weight_ref[...], offset], 0)
    blocks[0] = own

    pl.semaphore_wait(barrier, len(peers))

    def block_copy(t, to):
        return pltpu.make_async_remote_copy(
            src_ref=blocks.at[0], dst_ref=blocks.at[t], send_sem=send.at[t - 1],
            recv_sem=recv.at[t - 1], device_id=to, device_id_type=MESH,
        )

    for t in reversed(range(1, SAVED)):
        block_copy(t, visitor(*TILES[t - 1])).start()
    for t in range(SAVED, COUNT):
        block_copy(t, visitor(*TILES[t - 1])).start()

    root = jnp.sqrt(own[6:7])
    own_prep(own, root, ra, rb, cj)

    def times(k):
        total = jnp.float32(0.0)
        for r in range(shift_ref.shape[0]):
            total += jnp.where(shift_ref[r, g] == k, 1.0, 0.0)
            total += jnp.where(shift_ref[r, (g + k) % G] == G - k, 1.0, 0.0)
        return total

    times_of = {k: times(k) for k in range(1, G)}

    def spread(value, box, send_sem, recv_sem, peer, n):
        box[0] = value
        for i in range(1, n):
            pltpu.make_async_remote_copy(
                src_ref=box.at[0], dst_ref=box.at[i], send_sem=send_sem.at[i - 1],
                recv_sem=recv_sem.at[i - 1], device_id=peer(i), device_id_type=MESH,
            ).start()

    def gathered(box, send_sem, recv_sem, peer, n):
        for i in range(1, n):
            pltpu.make_async_remote_copy(
                src_ref=box.at[0], dst_ref=box.at[i], send_sem=send_sem.at[i - 1],
                recv_sem=recv_sem.at[i - 1], device_id=peer(i), device_id_type=MESH,
            ).wait()
        return functools.reduce(jnp.add, [box[i] for i in range(n)])

    boxes = (
        (box_a, send_a, recv_a, peer_a, G * ZH),
        (box_b, send_b, recv_b, peer_b, Y),
        (box_c, send_c, recv_c, peer_c, X),
    )
    xts, cts, abs_ = (xt0, xt1), (ct0, ct1), (ab0, ab1)

    def ready(t, odd, i):
        scale = jnp.float32(1.0)
        for j, (axis, k) in enumerate(TILES):
            if axis == "grp":
                scale = jnp.where(t == j + 1, times_of[k], scale)
        prepare(blocks[t], scale, xts[odd], cts[odd], fs, t)
        abs_[odd][i, 0] = dot(xts[odd][...], ra[...])
        abs_[odd][i, 1] = dot(xts[odd][...], rb[...])

    def arrive(t):
        block_copy(t, visitor("blk", 1)).wait_recv()

    def energy_stage(t, odd, i, after):
        arrive(t + 1)
        ready(t + 1, 1 - odd, after)
        energy_pass(cts[odd], cj, abs_[odd], i, qk, t, eacc)

    ready(0, 0, 0)

    def energies(s, carry):
        energy_stage(2 * s, 0, s, s)
        energy_stage(2 * s + 1, 1, s, s + 1)
        eacc[...] = eacc[...] * jnp.where(s == 0, 0.5, 1.0)
        return carry

    lax.fori_loop(0, SAVED // 2, energies, 0)
    energy_stage(SAVED - 1, 0, SAVED // 2, SAVED // 2)
    e = jnp.sum(eacc[...], 0, keepdims=True)
    spread(functools.reduce(jnp.add, [e[:, k : k + 128] for k in range(0, count, 128)]), *boxes[0])

    def gradients(s, carry):
        for odd in range(2):
            t = 2 * s + odd
            grad_pass(saved_values(abs_[odd], s, qk, t), co, fs, t, jnp.maximum(t - 1, 0), acc, count)
        return carry

    lax.fori_loop(0, SAVED // 2, gradients, 0)
    grad_pass(saved_values(ab0, SAVED // 2, qk, SAVED - 1), co, fs, SAVED - 1, SAVED - 2, acc, count)

    spread(gathered(*boxes[0]), *boxes[1])

    def full_stage(t, odd, i, after):
        grad_pass(full_values(cts[odd], cj, abs_[odd], i), co, fs, t, t - 1, acc, count)

    arrive(SAVED + 1)
    ready(SAVED + 1, 0, 0)
    full_stage(SAVED, 1, SAVED // 2, 0)

    def rest(s, carry):
        t = SAVED + 1 + 2 * s

        @pl.when(s == 1)
        def _():
            spread(gathered(*boxes[1]), *boxes[2])

        arrive(t + 1)
        ready(t + 1, 1, 0)
        full_stage(t, 0, 0, 0)

        @pl.when(t + 2 < COUNT)
        def _():
            arrive(t + 2)

        ready(jnp.minimum(t + 2, COUNT - 1), 0, 0)
        full_stage(t + 1, 1, 0, 0)
        return carry

    lax.fori_loop(0, (COUNT - SAVED) // 2, rest, 0)
    reduce_chunk(co, count // CHUNK - 1, fs, COUNT - 1, acc)

    s = [acc[m, 0:8, :] + acc[m, 8:16, :] + acc[m, 16:24, :] for m in range(3)]
    twice = 2.0 * root
    gn = rows_of((own[0:3] * s[0][6:7] - s[0][0:3]) * twice)
    gc = (own[3:6] * s[0][6:7] + s[1][3:6]) * twice - 4.0 * (own[0:3] * s[2][6:7] - s[2][0:3])
    gc = gc / 3.0
    g1 = 0.5 * jnp.concatenate(cross(e2, gn), 0)
    g2 = 0.5 * jnp.concatenate(cross(gn, e1), 0)
    total = jnp.zeros((16, verts), F)
    for k, gu in enumerate((gc - g1 - g2, gc + g1, gc + g2)):
        parts = jnp.concatenate([*split3(gu), jnp.zeros((7, count), F)], 0).astype(B)
        total += lax.dot_general(parts, hot[k], (((1,), (1,)), ((), ())), preferred_element_type=F)
    grad_ref[...] = (total[0:3] + total[3:6] + total[6:9]) * (1.0 / count)

    for t in range(1, COUNT):
        block_copy(t, visitor(*TILES[t - 1])).wait_send()
    energy_ref[0] = jnp.sum(gathered(*boxes[2])) * (1.0 / (count * count * G * blk_n))


def shards(vertices, faces, trial_step, accepted, face_weight, partner_shift):
    verts, count = vertices.shape[1], faces.shape[1]
    hbm = pl.BlockSpec(memory_space=pltpu.HBM)
    dma = pltpu.SemaphoreType.DMA
    vmem = pltpu.VMEM
    slots = (SAVED + 1) // 2
    return tuple(pl.pallas_call(
        kernel,
        out_shape=(jax.ShapeDtypeStruct((3, verts), F), jax.ShapeDtypeStruct((1,), F)),
        in_specs=[hbm] * 6,
        out_specs=(
            pl.BlockSpec(memory_space=pltpu.VMEM), pl.BlockSpec(memory_space=pltpu.SMEM)
        ),
        scratch_shapes=[
            vmem((3, verts), F), vmem((3, count), jnp.int32), vmem((3, verts), F),
            vmem((1, count), F), pltpu.SMEM((1,), jnp.int32),
            pltpu.SMEM(partner_shift.shape, jnp.int32), dma((6,)),
            vmem((COUNT, 8, count), F),
            vmem((3, verts, count), B),
            vmem((count, 48), B), vmem((count, 48), B),
            vmem((count, 8), F), vmem((count, 8), F),
            vmem((COUNT, 64, count), B),
            vmem((48, count), B), vmem((48, count), B),
            vmem((3, 8, count), F),
            vmem((slots, 2, count, count), F), vmem((slots, 2, count, count), F),
            vmem((SAVED, 2, count, count), F),
            vmem((count // CHUNK, 6, CHUNK, count), B),
            vmem((3, 32, count), F),
            vmem((8, count), F),
            vmem((G * ZH, 1, 128), F), vmem((Y, 1, 128), F), vmem((X, 1, 128), F),
            dma((COUNT - 1,)), dma((COUNT - 1,)),
            dma((G * ZH - 1,)), dma((G * ZH - 1,)),
            dma((Y - 1,)), dma((Y - 1,)),
            dma((X - 1,)), dma((X - 1,)),
        ],
        compiler_params=pltpu.CompilerParams(
            collective_id=0, has_side_effects=True, vmem_limit_bytes=48 << 20
        ),
    )(vertices, faces, trial_step, face_weight.reshape(1, count), accepted, partner_shift))


def solution(mesh):
    both = ("grp", "blk")
    placed = (P(None, both), P(None, both), P(None, both), P("grp"), P(both), P())
    return jax.shard_map(
        shards, mesh=mesh, in_specs=placed, out_specs=(P(None, both), P()), check_vma=False
    )
```

time: 45.1 us -> 48.9 us (1.084)
  local copies, waits for them, and re-layouts: 1.27 us -> 3.33 us
  Pallas kernels: 40.4 us -> 42.2 us
    unnamed x1 -> x11, local copies, waits for them, and re-layouts: 1.27 us -> 3.33 us
    pallas_call x1, Pallas kernels: 40.4 us -> 42.2 us  [shards(): pl.pallas_call(kernel, out_shape=(jax.ShapeDtypeStruct((3, verts), F), ja...]
where the time goes in v2:
time: 48.9 us; the launch traced here: 48.6 us
  Pallas kernels  42.2 us (86%)
  local copies, waits for them, and re-layouts  3.33 us (7%)
  between operations  3.01 us (6%)
    pallas_call x1, Pallas kernels, shards(): pl.pallas_call(kernel, out_shape=(jax.ShapeDtypeStruct((3, verts), F), ja...  42.2 us
    unnamed x11, local copies, waits for them, and re-layouts  3.33 us

profile of v2, /device:TPU:1, one launch (start us, length us, event | category | flops | bytes accessed | tf_op | source)
XLA Modules:
  0.0 48.6 jit_solution(3655637669096889661)
XLA Ops:
  0.6 0.0 copy-start.3
  1.3 0.0 copy-start.4
  1.3 0.0 copy-done.3
  1.3 0.7 %copy-done.4 = s32[2,4]{1,0:T(2,128)S(1)} copy-done((s32[2,4]{1,0:T(2,128)S(1)}, s32[2,4]{1,0:T(2,128)}, u32[]{:S(2)}) %copy-start.4) | copy-done | bytes 56
  2.0 0.0 copy-start
  2.0 0.7 %copy-done = s32[3,512]{1,0:T(4,128)S(1)} copy-done((s32[3,512]{1,0:T(4,128)S(1)}, s32[3,512]{1,0:T(4,128)}, u32[]{:S(2)}) %copy-start) | copy-done | bytes 6168
  2.7 0.0 copy-start.1
  2.7 0.7 %copy-done.1 = f32[3,256]{1,0:T(4,128)S(1)} copy-done((f32[3,256]{1,0:T(4,128)S(1)}, f32[3,256]{1,0:T(4,128)}, u32[]{:S(2)}) %copy-start.1) | copy-done | bytes 3096
  3.4 0.0 copy-start.2
  3.4 0.7 %copy-done.2 = f32[3,256]{1,0:T(4,128)S(1)} copy-done((f32[3,256]{1,0:T(4,128)S(1)}, f32[3,256]{1,0:T(4,128)}, u32[]{:S(2)}) %copy-start.2) | copy-done | bytes 3096
  4.1 42.2 %shard_map.77 = (f32[3,256]{1,0:T(4,128)S(1)}, f32[1]{0:T(128)}) custom-call(f32[3,256]{1,0:T(4,128)S(1)} %copy-done.1, s32[3,512]{1,0:T(4,128)S(1)} %copy-done, f32[3,256]{1,0:T(4,128)S(1)} %copy-done.2, f32[1,512]{1,0:T(1,128)S(1)} %bitcast.1, s32[1]{0:T(128)S(6)} %copy.10.acc_hbm, s32[2,4]{1,0:T(2,128)S(1)} %copy-done.4), custom_call_target="tpu_custom_call" | custom-call | tf_op jit(solution)/shard_map/pallas_call | solution.py:364
  46.3 0.6 %copy.11 = f32[3,256]{1,0:T(4,128)} copy(f32[3,256]{1,0:T(4,128)S(1)} %get-tuple-element.4) | data formatting | bytes 6144
Async XLA Ops:
  0.6 0.7 %copy-start.3 = (f32[512]{0:T(512)S(1)}, f32[512]{0:T(512)}, u32[]{:S(2)}) copy-start(f32[512]{0:T(512)} %param.10) | copy-start | bytes 6148
  1.3 0.7 %copy-start.4 = (s32[2,4]{1,0:T(2,128)S(1)}, s32[2,4]{1,0:T(2,128)}, u32[]{:S(2)}) copy-start(s32[2,4]{1,0:T(2,128)} %shift_hbm.1) | copy-start | bytes 100
  2.0 0.7 %copy-start = (s32[3,512]{1,0:T(4,128)S(1)}, s32[3,512]{1,0:T(4,128)}, u32[]{:S(2)}) copy-start(s32[3,512]{1,0:T(4,128)} %faces_hbm.1) | copy-start | bytes 18436
  2.7 0.7 %copy-start.1 = (f32[3,256]{1,0:T(4,128)S(1)}, f32[3,256]{1,0:T(4,128)}, u32[]{:S(2)}) copy-start(f32[3,256]{1,0:T(4,128)} %ver_hbm.1) | copy-start | bytes 9220
  3.4 0.7 %copy-start.2 = (f32[3,256]{1,0:T(4,128)S(1)}, f32[3,256]{1,0:T(4,128)}, u32[]{:S(2)}) copy-start(f32[3,256]{1,0:T(4,128)} %step_hbm.1) | copy-start | bytes 9220

commit v3 on v1

--- a/solution.py
+++ b/solution.py
@@ -15,6 +15,7 @@
 LANES = 256
 ROWS = 16
 MESH = pl.DeviceIdType.MESH
+Y, ZH, X, G = 8, 4, 4, 4
 
 TILES = (
     [("grp", 2), ("grp", 1)]
@@ -22,9 +23,10 @@
     + [("grp", 3)]
     + [("blk", -k) for k in range(1, HOPS + 1)]
 )
+COUNT = len(TILES) + 1
 HALF_AT = 2
 FULL_AT = 7
-Y, ZH, X, G = 8, 4, 4, 4
+PASS_AT = 9
 
 
 def split3(x):
@@ -62,15 +64,14 @@
         cj[k] = jnp.broadcast_to(own[k : k + 1], (8, n))
 
 
-def other_prep(blk, wrow, xt, ct, fs):
+def other_prep(blk, wrow, xt, ct, fs, slot):
     row = lax.broadcasted_iota(jnp.int32, blk.shape, 0)
     x = jnp.where(row == 6, 1.0, blk)
     h, m, low = split3(x)
-    tr = jnp.concatenate([h, h, h, m, m, low, blk, blk], 0).T
-    xt[...] = tr[:, :48].astype(B)
-    ct[...] = tr[:, 48:56]
+    xt[slot] = jnp.concatenate([h, h, h, m, m, low], 0).astype(B).T
+    ct[slot] = blk.T
     h, m, low = split3(x * wrow)
-    fs[...] = jnp.concatenate([h, m, low, jnp.zeros_like(low)], 0).astype(B)
+    fs[slot] = jnp.concatenate([h, m, low, jnp.zeros_like(low)], 0).astype(B)
 
 
 def pairs(ct, cj, ab, co, slot, base, r0):
@@ -133,9 +134,10 @@
 
 
 def kernel(
-    ver_ref, faces_ref, step_ref, weight_ref, acc_ref, shift_ref, grad_ref, energy_ref,
+    ver_hbm, faces_hbm, step_hbm, weight_hbm, acc_hbm, shift_hbm, grad_ref, energy_ref,
+    ver_ref, faces_ref, step_ref, weight_ref, acc_ref, shift_ref, in_sem,
     blocks, hot, xt, ct, fs, ra, rb, cj, ab, co, acc, part,
-    box_a, box_b, box_c, send, recv, send_a, recv_a, send_b, recv_b, send_c, recv_c,
+    box_a, box_b, send, recv, send_a, recv_a, send_b, recv_b,
 ):
     g = lax.axis_index("grp")
     b = lax.axis_index("blk")
@@ -147,10 +149,8 @@
         return (j // ZH, (y * ZH + j % ZH) * X + x)
 
     def peer_b(i):
-        return (g, (((y + i) % Y) * ZH + zh) * X + x)
-
-    def peer_c(i):
-        return (g, (y * ZH + zh) * X + (x + i) % X)
+        j = (y * X + x + i) % (Y * X)
+        return (g, ((j // X) * ZH + zh) * X + j % X)
 
     def visitor(axis, k):
         if axis == "grp":
@@ -159,10 +159,23 @@
 
     peers = [visitor(*t) for t in TILES if t[0] == "blk"]
     peers += [peer_a(i) for i in range(1, G * ZH)]
-    peers += [peer_b(i) for i in range(1, Y)] + [peer_c(i) for i in range(1, X)]
+    peers += [peer_b(i) for i in range(1, Y * X)]
     barrier = pltpu.get_barrier_semaphore()
     for p in peers:
         pl.semaphore_signal(barrier, inc=1, device_id=p, device_id_type=MESH)
+
+    loads = [
+        pltpu.make_async_copy(src, dst, in_sem.at[i])
+        for i, (src, dst) in enumerate((
+            (ver_hbm, ver_ref), (step_hbm, step_ref), (faces_hbm, faces_ref),
+            (weight_hbm, weight_ref), (acc_hbm, acc_ref), (shift_hbm, shift_ref),
+        ))
+    ]
+    for c in loads:
+        c.start()
+    acc[...] = jnp.zeros_like(acc)
+    for c in loads:
+        c.wait()
 
     verts, count = ver_ref.shape[1], faces_ref.shape[1]
     pos = ver_ref[...] + acc_ref[0].astype(F) * step_ref[...]
@@ -193,7 +206,6 @@
         block_copy(t + 1, visitor(*where)).start()
 
     own_prep(own, ra, rb, cj)
-    acc[...] = jnp.zeros_like(acc)
 
     def times(k):
         total = jnp.float32(0.0)
@@ -222,14 +234,21 @@
 
     boxes = (
         (box_a, send_a, recv_a, peer_a, G * ZH),
-        (box_b, send_b, recv_b, peer_b, Y),
-        (box_c, send_c, recv_c, peer_c, X),
+        (box_b, send_b, recv_b, peer_b, Y * X),
     )
 
+    def ready(t):
+        scale = jnp.float32(1.0)
+        for j, (axis, k) in enumerate(TILES):
+            if axis == "grp":
+                scale = jnp.where(t == j + 1, times_of[k], scale)
+        blk = blocks[t]
+        other_prep(blk, blk[6:7] * scale, xt, ct, fs, t % 2)
+
     def visit(t, carry):
-        @pl.when(t > 0)
+        @pl.when(t + 1 < COUNT)
         def _():
-            block_copy(t, visitor("blk", 1)).wait_recv()
+            block_copy(t + 1, visitor("blk", 1)).wait_recv()
 
         @pl.when(t == HALF_AT)
         def _():
@@ -239,24 +258,17 @@
         def _():
             spread(energy_of(own, acc) - 0.5 * part[...], *boxes[0])
 
-        @pl.when(t == FULL_AT + 2)
+        @pl.when(t == PASS_AT)
         def _():
             spread(gathered(*boxes[0]), *boxes[1])
 
-        @pl.when(t == FULL_AT + 4)
-        def _():
-            spread(gathered(*boxes[1]), *boxes[2])
-
-        blk = blocks[t]
-        scale = jnp.float32(1.0)
-        for i, (axis, k) in enumerate(TILES):
-            if axis == "grp":
-                scale = jnp.where(t == i + 1, times_of[k], scale)
-        other_prep(blk, blk[6:7] * scale, xt, ct, fs)
-        tile(xt, ct, fs, ra, rb, cj, ab, co, acc)
+        now = t % 2
+        tile(xt.at[now], ct.at[now], fs.at[now], ra, rb, cj, ab, co, acc)
+        ready(jnp.minimum(t + 1, COUNT - 1))
         return carry
 
-    lax.fori_loop(0, len(TILES) + 1, visit, 0)
+    ready(0)
+    lax.fori_loop(0, COUNT, visit, 0)
 
     s = sums_of(acc)
     twice = 2.0 * own[6:7]
@@ -273,40 +285,40 @@
 
     for t, where in enumerate(TILES):
         block_copy(t + 1, visitor(*where)).wait_send()
-    energy_ref[0] = jnp.sum(gathered(*boxes[2])) * (1.0 / (count * count * G * blk_n))
+    energy_ref[0] = jnp.sum(gathered(*boxes[1])) * (1.0 / (count * count * G * blk_n))
 
 
 def shards(vertices, faces, trial_step, accepted, face_weight, partner_shift):
     verts, count = vertices.shape[1], faces.shape[1]
-    vmem = pl.BlockSpec(memory_space=pltpu.VMEM)
-    smem = pl.BlockSpec(memory_space=pltpu.SMEM)
+    hbm = pl.BlockSpec(memory_space=pltpu.HBM)
     dma = pltpu.SemaphoreType.DMA
-    n = len(TILES)
+    vmem = pltpu.VMEM
     return tuple(pl.pallas_call(
         kernel,
         out_shape=(jax.ShapeDtypeStruct((3, verts), F), jax.ShapeDtypeStruct((1,), F)),
-        in_specs=[vmem] * 4 + [smem] * 2,
-        out_specs=(vmem, smem),
+        in_specs=[hbm] * 6,
+        out_specs=(
+            pl.BlockSpec(memory_space=pltpu.VMEM), pl.BlockSpec(memory_space=pltpu.SMEM)
+        ),
         scratch_shapes=[
-            pltpu.VMEM((n + 1, 8, count), F),
-            pltpu.VMEM((3, verts, count), B),
-            pltpu.VMEM((count, 48), B),
-            pltpu.VMEM((count, 8), F),
-            pltpu.VMEM((32, count), B),
-            pltpu.VMEM((48, count), B),
-            pltpu.VMEM((48, count), B),
-            pltpu.VMEM((3, 8, count), F),
-            pltpu.VMEM((2, 2, CHUNK, count), F),
-            pltpu.VMEM((2, 6, CHUNK, count), B),
-            pltpu.VMEM((3, 32, count), F),
-            pltpu.VMEM((1, 128), F),
-            pltpu.VMEM((G * ZH, 1, 128), F),
-            pltpu.VMEM((Y, 1, 128), F),
-            pltpu.VMEM((X, 1, 128), F),
-            dma((n,)), dma((n,)),
+            vmem((3, verts), F), vmem((3, count), jnp.int32), vmem((3, verts), F),
+            vmem((1, count), F), pltpu.SMEM((1,), jnp.int32),
+            pltpu.SMEM(partner_shift.shape, jnp.int32), dma((6,)),
+            vmem((COUNT, 8, count), F),
+            vmem((3, verts, count), B),
+            vmem((2, count, 48), B),
+            vmem((2, count, 8), F),
+            vmem((2, 32, count), B),
+            vmem((48, count), B), vmem((48, count), B),
+            vmem((3, 8, count), F),
+            vmem((2, 2, CHUNK, count), F),
+            vmem((2, 6, CHUNK, count), B),
+            vmem((3, 32, count), F),
+            vmem((1, 128), F),
+            vmem((G * ZH, 1, 128), F), vmem((Y * X, 1, 128), F),
+            dma((COUNT - 1,)), dma((COUNT - 1,)),
             dma((G * ZH - 1,)), dma((G * ZH - 1,)),
-            dma((Y - 1,)), dma((Y - 1,)),
-            dma((X - 1,)), dma((X - 1,)),
+            dma((Y * X - 1,)), dma((Y * X - 1,)),
         ],
         compiler_params=pltpu.CompilerParams(collective_id=0, has_side_effects=True),
     )(vertices, faces, trial_step, face_weight.reshape(1, count), accepted, partner_shift))

time: 45.1 us -> 44.9 us (level)
  no operation moved by 1% of the time
where the time goes in v3:
time: 44.9 us; the launch traced here: 44.7 us
  Pallas kernels  40.4 us (90%)
  between operations  3.05 us (7%)
  local copies, waits for them, and re-layouts  1.27 us (3%)
    pallas_call x1, Pallas kernels, shards(): pl.pallas_call(kernel, out_shape=(jax.ShapeDtypeStruct((3, verts), F), ja...  40.4 us
    unnamed x1, local copies, waits for them, and re-layouts  1.27 us

profile of v3, /device:TPU:1, one launch (start us, length us, event | category | flops | bytes accessed | tf_op | source)
XLA Modules:
  0.0 44.7 jit_solution(466107744445920904)
XLA Ops:
  1.3 40.4 %shard_map.77 = (f32[3,256]{1,0:T(4,128)}, f32[1]{0:T(128)}) custom-call(f32[3,256]{1,0:T(4,128)} %ver_hbm.1, s32[3,512]{1,0:T(4,128)} %faces_hbm.1, f32[3,256]{1,0:T(4,128)} %step_hbm.1, f32[1,512]{1,0:T(1,128)} %bitcast.1, s32[1]{0:T(128)S(6)} %copy.10.acc_hbm, s32[2,4]{1,0:T(2,128)} %shift_hbm.1), custom_call_target="tpu_custom_call" | custom-call | tf_op jit(solution)/shard_map/pallas_call | solution.py:296
  41.7 1.3 %copy.11 = f32[3,256]{1,0:T(4,128)} copy(f32[3,256]{1,0:T(4,128)} %get-tuple-element.4) | data formatting | bytes 6144

commit v4 on v3

--- a/solution.py
+++ b/solution.py
@@ -137,7 +137,7 @@
     ver_hbm, faces_hbm, step_hbm, weight_hbm, acc_hbm, shift_hbm, grad_ref, energy_ref,
     ver_ref, faces_ref, step_ref, weight_ref, acc_ref, shift_ref, in_sem,
     blocks, hot, xt, ct, fs, ra, rb, cj, ab, co, acc, part,
-    box_a, box_b, send, recv, send_a, recv_a, send_b, recv_b,
+    box_a, box_b, box_c, send, recv, send_a, recv_a, send_b, recv_b, send_c, recv_c,
 ):
     g = lax.axis_index("grp")
     b = lax.axis_index("blk")
@@ -149,8 +149,10 @@
         return (j // ZH, (y * ZH + j % ZH) * X + x)
 
     def peer_b(i):
-        j = (y * X + x + i) % (Y * X)
-        return (g, ((j // X) * ZH + zh) * X + j % X)
+        return (g, (((y + i) % Y) * ZH + zh) * X + x)
+
+    def peer_c(i):
+        return (g, (y * ZH + zh) * X + (x + i) % X)
 
     def visitor(axis, k):
         if axis == "grp":
@@ -159,7 +161,7 @@
 
     peers = [visitor(*t) for t in TILES if t[0] == "blk"]
     peers += [peer_a(i) for i in range(1, G * ZH)]
-    peers += [peer_b(i) for i in range(1, Y * X)]
+    peers += [peer_b(i) for i in range(1, Y)] + [peer_c(i) for i in range(1, X)]
     barrier = pltpu.get_barrier_semaphore()
     for p in peers:
         pl.semaphore_signal(barrier, inc=1, device_id=p, device_id_type=MESH)
@@ -234,7 +236,8 @@
 
     boxes = (
         (box_a, send_a, recv_a, peer_a, G * ZH),
-        (box_b, send_b, recv_b, peer_b, Y * X),
+        (box_b, send_b, recv_b, peer_b, Y),
+        (box_c, send_c, recv_c, peer_c, X),
     )
 
     def ready(t):
@@ -261,6 +264,10 @@
         @pl.when(t == PASS_AT)
         def _():
             spread(gathered(*boxes[0]), *boxes[1])
+
+        @pl.when(t == PASS_AT + 2)
+        def _():
+            spread(gathered(*boxes[1]), *boxes[2])
 
         now = t % 2
         tile(xt.at[now], ct.at[now], fs.at[now], ra, rb, cj, ab, co, acc)
@@ -285,7 +292,7 @@
 
     for t, where in enumerate(TILES):
         block_copy(t + 1, visitor(*where)).wait_send()
-    energy_ref[0] = jnp.sum(gathered(*boxes[1])) * (1.0 / (count * count * G * blk_n))
+    energy_ref[0] = jnp.sum(gathered(*boxes[2])) * (1.0 / (count * count * G * blk_n))
 
 
 def shards(vertices, faces, trial_step, accepted, face_weight, partner_shift):
@@ -315,10 +322,11 @@
             vmem((2, 6, CHUNK, count), B),
             vmem((3, 32, count), F),
             vmem((1, 128), F),
-            vmem((G * ZH, 1, 128), F), vmem((Y * X, 1, 128), F),
+            vmem((G * ZH, 1, 128), F), vmem((Y, 1, 128), F), vmem((X, 1, 128), F),
             dma((COUNT - 1,)), dma((COUNT - 1,)),
             dma((G * ZH - 1,)), dma((G * ZH - 1,)),
-            dma((Y * X - 1,)), dma((Y * X - 1,)),
+            dma((Y - 1,)), dma((Y - 1,)),
+            dma((X - 1,)), dma((X - 1,)),
         ],
         compiler_params=pltpu.CompilerParams(collective_id=0, has_side_effects=True),
     )(vertices, faces, trial_step, face_weight.reshape(1, count), accepted, partner_shift))

time: 44.9 us -> 44.6 us (level)
  Pallas kernels: 40.4 us -> 39.8 us
    pallas_call x1, Pallas kernels: 40.4 us -> 39.8 us  [shards(): pl.pallas_call(kernel, out_shape=(jax.ShapeDtypeStruct((3, verts), F), ja...]
where the time goes in v4:
time: 44.6 us; the launch traced here: 44.1 us
  Pallas kernels  39.8 us (89%)
  between operations  3.05 us (7%)
  local copies, waits for them, and re-layouts  1.27 us (3%)
    pallas_call x1, Pallas kernels, shards(): pl.pallas_call(kernel, out_shape=(jax.ShapeDtypeStruct((3, verts), F), ja...  39.8 us
    unnamed x1, local copies, waits for them, and re-layouts  1.27 us

profile of v4, /device:TPU:1, one launch (start us, length us, event | category | flops | bytes accessed | tf_op | source)
XLA Modules:
  0.0 44.1 jit_solution(6762293644135510613)
XLA Ops:
  1.3 39.8 %shard_map.77 = (f32[3,256]{1,0:T(4,128)}, f32[1]{0:T(128)}) custom-call(f32[3,256]{1,0:T(4,128)} %ver_hbm.1, s32[3,512]{1,0:T(4,128)} %faces_hbm.1, f32[3,256]{1,0:T(4,128)} %step_hbm.1, f32[1,512]{1,0:T(1,128)} %bitcast.1, s32[1]{0:T(128)S(6)} %copy.10.acc_hbm, s32[2,4]{1,0:T(2,128)} %shift_hbm.1), custom_call_target="tpu_custom_call" | custom-call | tf_op jit(solution)/shard_map/pallas_call | solution.py:303
  41.1 1.3 %copy.11 = f32[3,256]{1,0:T(4,128)} copy(f32[3,256]{1,0:T(4,128)} %get-tuple-element.4) | data formatting | bytes 6144
